TPU v7x, 32 devices: a whole 2x2x4 slice. The times are simulated.
32 devices in a mesh: grp: 2 (over x), area: 8 (over z, y), ctg: 2 (over core).
Axes of the slice: x: 2, y: 2, z: 4, core: 2. Of those that a mesh axis runs over, the one named last changes fastest.
Arguments:
- area_size: int32 [16], P(('grp', 'area')), parts along dimension 0, may hold values from 299 to 1024, as said below
- tie_peer: int32 [16, 42], P(('grp', 'area')), parts along dimension 0, may hold values from 0 to 7, as said below
- kkt_diag: float32 [16, 2, 1024], P(('grp', 'area'), 'ctg'), parts along dimension 0, may hold values from 0.5 to 1
- kkt_offdiag: float32 [16, 2, 1024, 1024], P(('grp', 'area'), 'ctg'), parts along dimension 0, may hold values from -0.1875 to 0.1875
- cost: float32 [16, 2, 1024, 256], P(('grp', 'area'), 'ctg'), parts along dimension 0, may hold values from -6 to 6
- consensus: float32 [16, 2, 1024, 256], P(('grp', 'area'), 'ctg'), parts along dimension 0, may hold values from -4 to 4
- dual: float32 [16, 2, 1024, 256], P(('grp', 'area'), 'ctg'), parts along dimension 0, may hold values from -4 to 4
- limit: float32 [16, 1024, 256], P(('grp', 'area')), parts along dimension 0, may hold values from 0.3 to 1.5
Outputs:
- agreed_out: float32 [16, 2, 1024, 256], P(('grp', 'area'), 'ctg'), parts along dimension 0
- dual_out: float32 [16, 2, 1024, 256], P(('grp', 'area'), 'ctg'), parts along dimension 0
There are 2 independent parts, one for each index of `grp`. A program takes and returns all parts, laid end to end along the dimension named above; each array names one. Nothing has to cross between parts.
Inputs may be any that keep to these rules, and one draw needn't show every extreme that they name: `area_size`: some area has exactly 1024 live slots. `tie_peer`: never the area itself; each area has exactly 6 tie slots to each other area.
All inputs are finite; a program needn't handle non-finite values.
Results may differ from a plain program's by a relative error of at most 0.0003.
Values sent between devices are 32-bit elements; how exact they have to be, the bound alone decides.
No kernel may reach another device: no remote copies, remote signals or barrier semaphores. Data moves between devices by JAX's collectives and lax.ppermute only.
A program may use at most 64 MiB of HBM per device.

v0:
```python
import jax
import jax.numpy as jnp
from jax import lax
from jax.sharding import PartitionSpec as P

GENS = 256
ITERS = 3


def tie_dest(peers, pair_lines):
    count = peers.shape[0]
    order = jnp.arange(count)
    same = (peers[:, None] == peers[None, :]) & (order[:, None] < order[None, :])
    rank = jnp.sum(same.astype(jnp.int32), axis=0)
    return peers * pair_lines + rank


def apply_rows(matrix, right_side):
    return jnp.dot(
        matrix, right_side, precision=lax.Precision.HIGHEST, preferred_element_type=jnp.float32
    )


def local(area_size, tie_peer, kkt_diag, kkt_offdiag, cost, consensus, dual, limit):
    areas = lax.axis_size("area")
    scenarios = lax.axis_size("ctg")
    peers = tie_peer[0]
    ties = peers.shape[0]
    pair_lines = ties // (areas - 1)
    dest = tie_dest(peers, pair_lines)
    slots = cost.shape[2]
    hours = cost.shape[3]
    shared = GENS + ties
    live = (jnp.arange(slots) < area_size[0]).astype(jnp.float32)[:, None]
    offdiag = kkt_offdiag[0, 0]
    diagonal = kkt_diag[0, 0][:, None]
    bound = limit[0]
    linear = cost[0, 0]
    agreed = consensus[0, 0]
    dual_var = dual[0, 0]
    for iteration in range(ITERS):
        right_side = live * (agreed - dual_var - linear)
        primal = live * (diagonal * right_side + apply_rows(offdiag, right_side))
        primal_top = primal[:shared]
        dual_top = dual_var[:shared]
        shifted = primal_top + dual_top
        gen_mean = lax.psum(shifted[:GENS], "ctg") / scenarios
        empty = jnp.zeros((areas * pair_lines, hours), jnp.float32)
        sent_primal = empty.at[dest].set(primal_top[GENS:])
        sent_dual = empty.at[dest].set(dual_top[GENS:])
        got_primal = lax.all_to_all(sent_primal, "area", split_axis=0, concat_axis=0, tiled=True)
        got_dual = lax.all_to_all(sent_dual, "area", split_axis=0, concat_axis=0, tiled=True)
        other = got_primal[dest] + got_dual[dest]
        top_part = jnp.concatenate([gen_mean, 0.5 * (shifted[GENS:] + other)], axis=0)
        averaged = jnp.concatenate([top_part, primal[shared:] + dual_var[shared:]], axis=0)
        agreed = live * jnp.clip(averaged, -bound, bound)
        dual_var = live * (dual_var + primal - agreed)
    return (agreed[None, None], dual_var[None, None])


def solution(mesh):
    return jax.shard_map(
        local,
        mesh=mesh,
        in_specs=(
            P(("grp", "area")),
            P(("grp", "area"), None),
            P(("grp", "area"), "ctg", None),
            P(("grp", "area"), "ctg", None, None),
            P(("grp", "area"), "ctg", None, None),
            P(("grp", "area"), "ctg", None, None),
            P(("grp", "area"), "ctg", None, None),
            P(("grp", "area"), None, None),
        ),
        out_specs=(P(("grp", "area"), "ctg", None, None), P(("grp", "area"), "ctg", None, None)),
        check_vma=False,
    )
```

profile of v0, /device:TPU:0, one launch (start us, length us, event | category | flops | bytes accessed | tf_op | source)
XLA Modules:
  0.0 138.7 jit_solution(8805056950843362891)
XLA Ops:
  7.2 0.8 convert_reduce_fusion
  8.0 0.7 fusion.85
  8.6 1.0 scatter_custom_fusion.1
  10.3 7.3 %all-to-all-start.1 = ((f32[8,6,256]{2,1,0:T(8,128)}), f32[8,6,256]{2,1,0:T(8,128)S(1)}, u32[]{:S(2)}, u32[]{:S(2)}) async-start(f32[8,6,256]{2,1,0:T(8,128)} %all_to_all.51), calls=%async_computation.1 | async-start | bytes 131072 | tf_op jit(solution)/shard_map/all_to_all | solution.py:52
  18.3 7.7 %fusion.12 = f32[1024,256]{1,0:T(8,128)S(1)} fusion(f32[1,1,1024,1024]{3,2,1,0:T(8,128)} %param.11, f32[1,1,1024,256]{3,2,1,0:T(8,128)} %param.12, f32[1,1,1024,256]{3,2,1,0:T(8,128)} %param.14, f32[1,1,1024,256]{3,2,1,0:T(8,128)} %param.13, f32[1024]{0:T(1024)} %bitcast.144, f32[1024]{0:T(1024)S(1)} %fusion.84), kind=kOutput, calls=%fused_computation.20 | convolution fusion | flops 3223584768 | bytes 8396800 | tf_op jit(solution)/shard_map/dot_general | solution.py:19
  26.0 1.0 copy-done.5
  27.0 0.7 slice.127
  27.8 1.3 slice_add_fusion.2
  29.1 1.0 scatter_custom_fusion
  30.1 0.6 all_to_all.48
  30.8 6.0 %all-to-all-start = ((f32[8,6,256]{2,1,0:T(8,128)}), f32[8,6,256]{2,1,0:T(8,128)S(1)}, u32[]{:S(2)}, u32[]{:S(2)}) async-start(f32[8,6,256]{2,1,0:T(8,128)} %all_to_all.48), calls=%async_computation | async-start | bytes 131072 | tf_op jit(solution)/shard_map/all_to_all | solution.py:51
  37.4 6.3 %all-to-all-done = f32[8,6,256]{2,1,0:T(8,128)S(1)} async-done(((f32[8,6,256]{2,1,0:T(8,128)}), f32[8,6,256]{2,1,0:T(8,128)S(1)}, u32[]{:S(2)}, u32[]{:S(2)}) %all-to-all-start) | async-done | bytes 49184 | tf_op jit(solution)/shard_map/all_to_all | solution.py:51
  44.3 3.3 %all-reduce.4.cloned.1.call-done = f32[256,256]{1,0:T(8,128)} async-done(((f32[256,256]{1,0:T(8,128)}), f32[256,256]{1,0:T(8,128)}) %all-reduce.4.cloned.1.call-update) | async-done | bytes 262160 | tf_op jit(solution)/shard_map/psum | solution.py:47
  47.5 1.1 broadcast_multiply_fusion.2
  48.7 2.1 %fusion.50 = f32[1024,256]{1,0:T(8,128)S(1)} fusion(f32[1024,256]{1,0:T(8,128)} %copy-done.5, f32[1,1,1024,256]{3,2,1,0:T(8,128)} %param.14, f32[1024]{0:T(1024)S(1)} %fusion.84, f32[726,256]{1,0:T(8,128)S(1)} %slice_add_fusion.2, f32[42,256]{1,0:T(8,128)S(1)} %fusion.73, f32[256,256]{1,0:T(8,128)S(1)} %broadcast_multiply_fusion.2, ...), kind=kLoop, calls=%fused_computation.53 | loop fusion | flops 2359296 | bytes 5246976 | tf_op jit(solution)/shard_map/mul | solution.py:57
  50.8 6.5 %fusion.21 = f32[1024,256]{1,0:T(8,128)} fusion(f32[1,1,1024,1024]{3,2,1,0:T(8,128)S(1)} %copy-done, f32[1,1,1024,256]{3,2,1,0:T(8,128)} %param.12, f32[1024,256]{1,0:T(8,128)S(1)} %fusion.50, f32[1024]{0:T(1024)S(1)} %bitcast.145, f32[1024]{0:T(1024)S(1)} %fusion.84, f32[726,256]{1,0:T(8,128)S(1)} %slice_add_fusion.2, f32[42,256]{1,0:T(8,128)S(1)} %fusion.73, ...), kind=kOutput, calls=%fused_computation.23 | convolution fusion | flops 3226730496 | bytes 9445376 | tf_op jit(solution)/shard_map/dot_general | solution.py:19
  57.4 1.0 scatter_custom_fusion.2
  58.4 0.6 all_to_all.54
  59.0 5.8 %all-to-all-start.2 = ((f32[8,6,256]{2,1,0:T(8,128)}), f32[8,6,256]{2,1,0:T(8,128)S(1)}, u32[]{:S(2)}, u32[]{:S(2)}) async-start(f32[8,6,256]{2,1,0:T(8,128)} %all_to_all.54), calls=%async_computation.2 | async-start | bytes 131072 | tf_op jit(solution)/shard_map/all_to_all | solution.py:51
  64.9 1.0 slice_add_fusion.4
  65.9 0.7 scatter_custom_fusion.3
  67.3 0.7 slice.133
  68.0 3.7 %all-to-all-done.2 = f32[8,6,256]{2,1,0:T(8,128)S(1)} async-done(((f32[8,6,256]{2,1,0:T(8,128)}), f32[8,6,256]{2,1,0:T(8,128)S(1)}, u32[]{:S(2)}, u32[]{:S(2)}) %all-to-all-start.2) | async-done | bytes 49184 | tf_op jit(solution)/shard_map/all_to_all | solution.py:51
  71.8 3.5 %all-to-all-start.3 = ((f32[8,6,256]{2,1,0:T(8,128)}), f32[8,6,256]{2,1,0:T(8,128)S(1)}, u32[]{:S(2)}, u32[]{:S(2)}) async-start(f32[8,6,256]{2,1,0:T(8,128)} %all_to_all.57), calls=%async_computation.3 | async-start | bytes 131072 | tf_op jit(solution)/shard_map/all_to_all | solution.py:52
  75.3 2.1 %slice_add_fusion.1 = f32[726,256]{1,0:T(8,128)} fusion(f32[1024,256]{1,0:T(8,128)S(1)} %fusion.50, f32[1024,256]{1,0:T(8,128)} %fusion.21), kind=kLoop, calls=%fused_computation.63 | loop fusion | flops 185856 | bytes 2230272 | tf_op jit(solution)/shard_map/add | solution.py:55
  78.0 3.9 %all-to-all-done.3 = f32[8,6,256]{2,1,0:T(8,128)S(1)} async-done(((f32[8,6,256]{2,1,0:T(8,128)}), f32[8,6,256]{2,1,0:T(8,128)S(1)}, u32[]{:S(2)}, u32[]{:S(2)}) %all-to-all-start.3) | async-done | bytes 49184 | tf_op jit(solution)/shard_map/all_to_all | solution.py:52
  82.6 5.1 %all-reduce.6.cloned.1.call-done = f32[256,256]{1,0:T(8,128)} async-done(((f32[256,256]{1,0:T(8,128)}), f32[256,256]{1,0:T(8,128)}) %all-reduce.6.cloned.1.call-update) | async-done | bytes 262160 | tf_op jit(solution)/shard_map/psum | solution.py:47
  87.7 1.1 broadcast_multiply_fusion.1
  88.9 2.3 %subtract_multiply_fusion = f32[1024,256]{1,0:T(8,128)S(1)} fusion(f32[1024,256]{1,0:T(8,128)S(1)} %fusion.50, f32[1024,256]{1,0:T(8,128)} %fusion.21, f32[1024]{0:T(1024)S(1)} %fusion.84, f32[726,256]{1,0:T(8,128)} %slice_add_fusion.1, f32[42,256]{1,0:T(8,128)S(1)} %fusion.70, f32[256,256]{1,0:T(8,128)S(1)} %broadcast_multiply_fusion.1, ...), kind=kLoop, calls=%fused_computation.57 | loop fusion | flops 2359296 | bytes 5246976 | tf_op jit(solution)/shard_map/mul | solution.py:57
  91.2 5.6 %fusion.30 = f32[1024,256]{1,0:T(8,128)S(1)} fusion(f32[1,1,1024,1024]{3,2,1,0:T(8,128)S(1)} %copy-done.1, f32[1,1,1024,256]{3,2,1,0:T(8,128)} %param.12, f32[1024,256]{1,0:T(8,128)S(1)} %subtract_multiply_fusion, f32[1024]{0:T(1024)S(1)} %bitcast.146, f32[1024]{0:T(1024)S(1)} %fusion.84, f32[726,256]{1,0:T(8,128)S(1)} %copy-done.3, ...), kind=kOutput, calls=%fused_computation.26 | convolution fusion | flops 3226730496 | bytes 9445376 | tf_op jit(solution)/shard_map/dot_general | solution.py:19
  96.8 0.7 scatter_custom_fusion.4
  97.5 0.6 all_to_all.60
  98.2 5.8 %all-to-all-start.4 = ((f32[8,6,256]{2,1,0:T(8,128)}), f32[8,6,256]{2,1,0:T(8,128)}, u32[]{:S(2)}, u32[]{:S(2)}) async-start(f32[8,6,256]{2,1,0:T(8,128)} %all_to_all.60), calls=%async_computation.4 | async-start | bytes 131072 | tf_op jit(solution)/shard_map/all_to_all | solution.py:51
  104.1 0.7 scatter_custom_fusion.5
  105.5 0.7 slice.141
  106.2 4.8 %all-to-all-done.4 = f32[8,6,256]{2,1,0:T(8,128)} async-done(((f32[8,6,256]{2,1,0:T(8,128)}), f32[8,6,256]{2,1,0:T(8,128)}, u32[]{:S(2)}, u32[]{:S(2)}) %all-to-all-start.4) | async-done | bytes 49184 | tf_op jit(solution)/shard_map/all_to_all | solution.py:51
  111.0 4.0 %all-to-all-start.5 = ((f32[8,6,256]{2,1,0:T(8,128)}), f32[8,6,256]{2,1,0:T(8,128)}, u32[]{:S(2)}, u32[]{:S(2)}) async-start(f32[8,6,256]{2,1,0:T(8,128)} %all_to_all.63), calls=%async_computation.5 | async-start | bytes 131072 | tf_op jit(solution)/shard_map/all_to_all | solution.py:52
  115.0 1.0 slice_add_fusion
  116.0 0.8 all_to_all.62
  116.8 1.2 gather_fusion.4
  118.0 3.9 %all-to-all-done.5 = f32[8,6,256]{2,1,0:T(8,128)} async-done(((f32[8,6,256]{2,1,0:T(8,128)}), f32[8,6,256]{2,1,0:T(8,128)}, u32[]{:S(2)}, u32[]{:S(2)}) %all-to-all-start.5) | async-done | bytes 49184 | tf_op jit(solution)/shard_map/all_to_all | solution.py:52
  121.9 0.8 all_to_all.65
  122.7 1.2 gather_fusion.5
  124.0 0.8 fusion.65
  124.8 2.5 %all-reduce.8.cloned.1.call-done = f32[256,256]{1,0:T(8,128)} async-done(((f32[256,256]{1,0:T(8,128)}), f32[256,256]{1,0:T(8,128)}) %all-reduce.8.cloned.1.call-update) | async-done | bytes 262160 | tf_op jit(solution)/shard_map/psum | solution.py:47
  127.3 1.1 broadcast_multiply_fusion
  128.4 2.5 %fusion.43 = f32[1,1,1024,256]{3,2,1,0:T(8,128)} fusion(f32[726,256]{1,0:T(8,128)} %slice_add_fusion, f32[42,256]{1,0:T(8,128)S(1)} %fusion.65, f32[256,256]{1,0:T(8,128)S(1)} %get-tuple-element.8, f32[1,1024,256]{2,1,0:T(8,128)S(1)} %copy-done.2, f32[1024,256]{1,0:T(8,128)S(1)} %subtract_multiply_fusion, f32[1024,256]{1,0:T(8,128)S(1)} %fusion.30, ...), kind=kLoop, calls=%fused_computation.41 | loop fusion | flops 2359296 | bytes 5246976 | tf_op jit(solution)/shard_map/broadcast_in_dim | solution.py:58
  130.9 1.3 fusion.38
  (39 shorter events, 4.7 us)
Async XLA Ops:
  10.3 20.5 %all-to-all-start.1 = ((f32[8,6,256]{2,1,0:T(8,128)}), f32[8,6,256]{2,1,0:T(8,128)S(1)}, u32[]{:S(2)}, u32[]{:S(2)}) async-start(f32[8,6,256]{2,1,0:T(8,128)} %all_to_all.51), calls=%async_computation.1 | async-start | bytes 131072 | tf_op jit(solution)/shard_map/all_to_all | solution.py:52
  17.6 29.9 %all-reduce.4.cloned.1.call-start = ((), (), s32[]{:S(2)}) async-start(), calls=%async_computation.6 | async-start | bytes 524288 | tf_op jit(solution)/shard_map/psum | solution.py:47
  18.3 8.7 %copy-start.4 = (f32[1,1,1024,256]{3,2,1,0:T(8,128)S(1)}, f32[1,1,1024,256]{3,2,1,0:T(8,128)}, u32[]{:S(2)}) copy-start(f32[1,1,1024,256]{3,2,1,0:T(8,128)} %param.14) | copy-start | bytes 3145732
  26.0 1.0 copy-start.5
  27.0 21.7 %copy-start.2 = (f32[1,1024,256]{2,1,0:T(8,128)S(1)}, f32[1,1024,256]{2,1,0:T(8,128)}, u32[]{:S(2)}) copy-start(f32[1,1024,256]{2,1,0:T(8,128)} %param.15) | copy-start | bytes 3145732
  29.1 21.7 %copy-start.7 = (f32[1,1,1024]{2,1,0:T(1,128)S(1)}, f32[1,1,1024]{2,1,0:T(1,128)}, u32[]{:S(2)}) copy-start(f32[1,1,1024]{2,1,0:T(1,128)} %param.10) | copy-start | bytes 12292
  30.8 12.9 %all-to-all-start = ((f32[8,6,256]{2,1,0:T(8,128)}), f32[8,6,256]{2,1,0:T(8,128)S(1)}, u32[]{:S(2)}, u32[]{:S(2)}) async-start(f32[8,6,256]{2,1,0:T(8,128)} %all_to_all.48), calls=%async_computation | async-start | bytes 131072 | tf_op jit(solution)/shard_map/all_to_all | solution.py:51
  47.5 3.3 %copy-start = (f32[1,1,1024,1024]{3,2,1,0:T(8,128)S(1)}, f32[1,1,1024,1024]{3,2,1,0:T(8,128)}, u32[]{:S(2)}) copy-start(f32[1,1,1024,1024]{3,2,1,0:T(8,128)} %param.11) | copy-start | bytes 12582916
  59.0 12.7 %all-to-all-start.2 = ((f32[8,6,256]{2,1,0:T(8,128)}), f32[8,6,256]{2,1,0:T(8,128)S(1)}, u32[]{:S(2)}, u32[]{:S(2)}) async-start(f32[8,6,256]{2,1,0:T(8,128)} %all_to_all.54), calls=%async_computation.2 | async-start | bytes 131072 | tf_op jit(solution)/shard_map/all_to_all | solution.py:51
  64.8 22.9 %all-reduce.6.cloned.1.call-start = ((), (), s32[]{:S(2)}) async-start(), calls=%async_computation.7 | async-start | bytes 524288 | tf_op jit(solution)/shard_map/psum | solution.py:47
  71.8 10.2 %all-to-all-start.3 = ((f32[8,6,256]{2,1,0:T(8,128)}), f32[8,6,256]{2,1,0:T(8,128)S(1)}, u32[]{:S(2)}, u32[]{:S(2)}) async-start(f32[8,6,256]{2,1,0:T(8,128)} %all_to_all.57), calls=%async_computation.3 | async-start | bytes 131072 | tf_op jit(solution)/shard_map/all_to_all | solution.py:52
  87.7 3.4 %copy-start.1 = (f32[1,1,1024,1024]{3,2,1,0:T(8,128)S(1)}, f32[1,1,1024,1024]{3,2,1,0:T(8,128)}, u32[]{:S(2)}) copy-start(f32[1,1,1024,1024]{3,2,1,0:T(8,128)} %param.11) | copy-start | bytes 12582916
  87.7 3.4 %copy-start.3 = (f32[726,256]{1,0:T(8,128)S(1)}, f32[726,256]{1,0:T(8,128)}, u32[]{:S(2)}) copy-start(f32[726,256]{1,0:T(8,128)} %slice_add_fusion.1) | copy-start | bytes 2230276
  98.2 12.8 %all-to-all-start.4 = ((f32[8,6,256]{2,1,0:T(8,128)}), f32[8,6,256]{2,1,0:T(8,128)}, u32[]{:S(2)}, u32[]{:S(2)}) async-start(f32[8,6,256]{2,1,0:T(8,128)} %all_to_all.60), calls=%async_computation.4 | async-start | bytes 131072 | tf_op jit(solution)/shard_map/all_to_all | solution.py:51
  104.0 23.3 %all-reduce.8.cloned.1.call-start = ((), (), s32[]{:S(2)}) async-start(), calls=%async_computation.8 | async-start | bytes 524288 | tf_op jit(solution)/shard_map/psum | solution.py:47
  111.0 10.9 %all-to-all-start.5 = ((f32[8,6,256]{2,1,0:T(8,128)}), f32[8,6,256]{2,1,0:T(8,128)}, u32[]{:S(2)}, u32[]{:S(2)}) async-start(f32[8,6,256]{2,1,0:T(8,128)} %all_to_all.63), calls=%async_computation.5 | async-start | bytes 131072 | tf_op jit(solution)/shard_map/all_to_all | solution.py:52
  127.3 3.5 %copy-start.6 = (f32[726,256]{1,0:T(8,128)S(1)}, f32[726,256]{1,0:T(8,128)}, u32[]{:S(2)}) copy-start(f32[726,256]{1,0:T(8,128)} %slice_add_fusion) | copy-start | bytes 2230276
Sparse Core Ops, SparseCore 0:
  27.9 19.5 all-reduce.3
  68.1 19.5 all-reduce.5
  107.7 19.5 all-reduce.7
where the time goes:
time: 140 us; the launch traced here: 139 us
  waiting for transfers between devices  33.6 us (24%)
  starting transfers between devices  32.5 us (23%)
  matrix products  19.9 us (14%)
  other arithmetic  19.3 us (14%)
  local copies, waits for them, and re-layouts  18.8 us (13%)
  between operations  14.6 us (10%)
    dot_general x3, matrix products, apply_rows(): jnp.dot(matrix, right_side, precision=lax.Precision.HIGHEST, preferred_el...  19.9 us
    all_to_all x3, starting transfers between devices, local(): lax.all_to_all(sent_primal, 'area', split_axis=0, concat_axis=0, tiled=True)  17.6 us
    all_to_all x3, starting transfers between devices, local(): lax.all_to_all(sent_dual, 'area', split_axis=0, concat_axis=0, tiled=True)  14.8 us
    all_to_all x3, waiting for transfers between devices, local(): lax.all_to_all(sent_primal, 'area', split_axis=0, concat_axis=0, tiled=True)  14.8 us
    psum x3, waiting for transfers between devices, local(): gen_mean = lax.psum(shifted[:GENS], 'ctg') / scenarios  10.9 us
    all_to_all x3, waiting for transfers between devices, local(): lax.all_to_all(sent_dual, 'area', split_axis=0, concat_axis=0, tiled=True)  7.78 us
    gather x6, local copies, waits for them, and re-layouts, local(): other = got_primal[dest] + got_dual[dest]  4.91 us
    mul x2, other arithmetic, local(): dual_var = live * (dual_var + primal - agreed)  4.41 us
  transfers between devices with their start and end apart: 9, of which 8 were waited for; matrix products, arithmetic and copies ran while one was open for 17% of the time, Pallas kernels for 0%

commit v1 on v0

--- a/solution.py
+++ b/solution.py
@@ -44,7 +44,7 @@
         primal_top = primal[:shared]
         dual_top = dual_var[:shared]
         shifted = primal_top + dual_top
-        gen_mean = lax.psum(shifted[:GENS], "ctg") / scenarios
+        gen_mean = jnp.sum(lax.all_gather(shifted[:GENS], "ctg"), axis=0) / scenarios
         empty = jnp.zeros((areas * pair_lines, hours), jnp.float32)
         sent_primal = empty.at[dest].set(primal_top[GENS:])
         sent_dual = empty.at[dest].set(dual_top[GENS:])

time: 140 us -> 117 us (0.84)
  waiting for transfers between devices: 33.6 us -> 19.8 us
  between operations: 14.6 us -> 1.59 us
  blocking collectives: 0 us -> 6.68 us
  starting transfers between devices: 32.5 us -> 28.1 us
  other arithmetic: 19.3 us -> 22.9 us
    psum x3 -> x0, waiting for transfers between devices: 10.9 us -> none  [local(): gen_mean = lax.psum(shifted[:GENS], 'ctg') / scenarios]
    all_gather x0 -> x3, blocking collectives: none -> 6.68 us  [local(): lax.all_gather(shifted[:GENS], 'ctg')]
    all_to_all x3, starting transfers between devices: 17.6 us -> 13.3 us  [local(): lax.all_to_all(sent_primal, 'area', split_axis=0, concat_axis=0, tiled=True)]
    reduce_sum x0 -> x3, other arithmetic: none -> 3.25 us  [local(): jnp.sum(lax.all_gather(shifted[:GENS], 'ctg'), axis=0) / scenarios]
    all_to_all x3, waiting for transfers between devices: 14.8 us -> 11.7 us  [local(): lax.all_to_all(sent_primal, 'area', split_axis=0, concat_axis=0, tiled=True)]
    slice x3, local copies, waits for them, and re-layouts: 2.15 us -> 0.05 us  [local(): shifted[:GENS]]
  transfers between devices with their start and end apart: 9 -> 6, of which waited for: 8 -> 5; matrix products, arithmetic and copies ran while one was open for 17% -> 16% of each run, Pallas kernels for 0% -> 0%
where the time goes in v1:
time: 117 us; the launch traced here: 116 us
  starting transfers between devices  28.1 us (24%)
  other arithmetic  22.9 us (20%)
  waiting for transfers between devices  19.8 us (17%)
  matrix products  18.6 us (16%)
  local copies, waits for them, and re-layouts  18.1 us (15%)
  blocking collectives  6.68 us (6%)
  between operations  1.59 us (1%)
    dot_general x3, matrix products, apply_rows(): jnp.dot(matrix, right_side, precision=lax.Precision.HIGHEST, preferred_el...  18.6 us
    all_to_all x3, starting transfers between devices, local(): lax.all_to_all(sent_dual, 'area', split_axis=0, concat_axis=0, tiled=True)  14.8 us
    all_to_all x3, starting transfers between devices, local(): lax.all_to_all(sent_primal, 'area', split_axis=0, concat_axis=0, tiled=True)  13.3 us
    all_to_all x3, waiting for transfers between devices, local(): lax.all_to_all(sent_primal, 'area', split_axis=0, concat_axis=0, tiled=True)  11.7 us
    all_to_all x3, waiting for transfers between devices, local(): lax.all_to_all(sent_dual, 'area', split_axis=0, concat_axis=0, tiled=True)  8.12 us
    all_gather x3, blocking collectives, local(): lax.all_gather(shifted[:GENS], 'ctg')  6.68 us
    gather x6, local copies, waits for them, and re-layouts, local(): other = got_primal[dest] + got_dual[dest]  4.92 us
    mul x2, other arithmetic, local(): dual_var = live * (dual_var + primal - agreed)  4.38 us
  transfers between devices with their start and end apart: 6, of which 5 were waited for; matrix products, arithmetic and copies ran while one was open for 16% of the time, Pallas kernels for 0%

profile of v1, /device:TPU:0, one launch (start us, length us, event | category | flops | bytes accessed | tf_op | source)
XLA Modules:
  0.0 115.8 jit_solution(7200170239035523543)
XLA Ops:
  0.6 0.8 convert_reduce_fusion
  1.5 0.7 fusion.85
  2.1 1.0 scatter_custom_fusion.1
  3.7 7.3 %all-to-all-start.1 = ((f32[8,6,256]{2,1,0:T(8,128)}), f32[8,6,256]{2,1,0:T(8,128)S(1)}, u32[]{:S(2)}, u32[]{:S(2)}) async-start(f32[8,6,256]{2,1,0:T(8,128)} %all_to_all.51), calls=%async_computation.1 | async-start | bytes 131072 | tf_op jit(solution)/shard_map/all_to_all | solution.py:52
  11.7 7.7 %fusion.12 = f32[1024,256]{1,0:T(8,128)S(1)} fusion(f32[1,1,1024,1024]{3,2,1,0:T(8,128)} %param.11, f32[1,1,1024,256]{3,2,1,0:T(8,128)} %param.12, f32[1,1,1024,256]{3,2,1,0:T(8,128)} %param.14, f32[1,1,1024,256]{3,2,1,0:T(8,128)} %param.13, f32[1024]{0:T(1024)} %bitcast.150, f32[1024]{0:T(1024)S(1)} %fusion.84), kind=kOutput, calls=%fused_computation.20 | convolution fusion | flops 3223584768 | bytes 8396800 | tf_op jit(solution)/shard_map/dot_general | solution.py:19
  20.3 2.2 %all-gather = f32[512,256]{1,0:T(8,128)S(1)} all-gather(f32[256,256]{1,0:T(8,128)S(1)} %slice.127), channel_id=2, replica_groups=mesh['grp'=2,'area'=8,'ctg'=2] {'ctg'}, dimensions={0}, use_global_device_ids=true | all-gather | bytes 786432 | tf_op jit(solution)/shard_map/all_gather | solution.py:47
  22.5 0.7 reduce_sum.38
  23.2 1.0 broadcast_multiply_fusion.2
  24.2 0.7 scatter_custom_fusion
  24.9 0.6 all_to_all.48
  25.6 6.0 %all-to-all-start = ((f32[8,6,256]{2,1,0:T(8,128)}), f32[8,6,256]{2,1,0:T(8,128)S(1)}, u32[]{:S(2)}, u32[]{:S(2)}) async-start(f32[8,6,256]{2,1,0:T(8,128)} %all_to_all.48), calls=%async_computation | async-start | bytes 131072 | tf_op jit(solution)/shard_map/all_to_all | solution.py:51
  32.2 6.3 %all-to-all-done = f32[8,6,256]{2,1,0:T(8,128)S(1)} async-done(((f32[8,6,256]{2,1,0:T(8,128)}), f32[8,6,256]{2,1,0:T(8,128)S(1)}, u32[]{:S(2)}, u32[]{:S(2)}) %all-to-all-start) | async-done | bytes 49184 | tf_op jit(solution)/shard_map/all_to_all | solution.py:51
  39.1 1.0 fusion.73
  40.1 2.4 %fusion.50 = f32[1024,256]{1,0:T(8,128)S(1)} fusion(f32[1024,256]{1,0:T(8,128)} %copy-done.4, f32[1,1,1024,256]{3,2,1,0:T(8,128)} %param.14, f32[1024]{0:T(1024)S(1)} %fusion.84, f32[726,256]{1,0:T(8,128)S(1)} %slice_add_fusion.2, f32[42,256]{1,0:T(8,128)S(1)} %fusion.73, f32[256,256]{1,0:T(8,128)S(1)} %broadcast_multiply_fusion.2, ...), kind=kLoop, calls=%fused_computation.53 | loop fusion | flops 2359296 | bytes 5246976 | tf_op jit(solution)/shard_map/mul | solution.py:57
  42.6 4.9 %fusion.21 = f32[1024,256]{1,0:T(8,128)} fusion(f32[1,1,1024,1024]{3,2,1,0:T(8,128)S(1)} %copy-done, f32[1,1,1024,256]{3,2,1,0:T(8,128)S(1)} %copy-done.5, f32[1024,256]{1,0:T(8,128)S(1)} %fusion.50, f32[1024]{0:T(1024)S(1)} %bitcast.151, f32[1024]{0:T(1024)S(1)} %fusion.84, f32[726,256]{1,0:T(8,128)S(1)} %slice_add_fusion.2, f32[42,256]{1,0:T(8,128)S(1)} %fusion.73, ...), kind=kOutput, calls=%fused_computation.23 | convolution fusion | flops 3226730496 | bytes 9445376 | tf_op jit(solution)/shard_map/dot_general | solution.py:19
  47.5 0.7 scatter_custom_fusion.3
  48.2 1.0 scatter_custom_fusion.2
  49.3 1.0 slice_add_fusion.4
  50.3 2.1 %slice_add_fusion.1 = f32[726,256]{1,0:T(8,128)} fusion(f32[1024,256]{1,0:T(8,128)S(1)} %fusion.50, f32[1024,256]{1,0:T(8,128)} %fusion.21), kind=kLoop, calls=%fused_computation.63 | loop fusion | flops 185856 | bytes 2230272 | tf_op jit(solution)/shard_map/add | solution.py:55
  52.4 0.6 all_to_all.54
  53.0 3.3 %all-to-all-start.2 = ((f32[8,6,256]{2,1,0:T(8,128)}), f32[8,6,256]{2,1,0:T(8,128)S(1)}, u32[]{:S(2)}, u32[]{:S(2)}) async-start(f32[8,6,256]{2,1,0:T(8,128)} %all_to_all.54), calls=%async_computation.2 | async-start | bytes 131072 | tf_op jit(solution)/shard_map/all_to_all | solution.py:51
  57.0 2.2 %all-gather.1 = f32[512,256]{1,0:T(8,128)S(1)} all-gather(f32[256,256]{1,0:T(8,128)S(1)} %slice.133), channel_id=3, replica_groups=mesh['grp'=2,'area'=8,'ctg'=2] {'ctg'}, dimensions={0}, use_global_device_ids=true | all-gather | bytes 786432 | tf_op jit(solution)/shard_map/all_gather | solution.py:47
  59.2 0.7 reduce_sum.41
  59.9 3.3 %all-to-all-done.2 = f32[8,6,256]{2,1,0:T(8,128)S(1)} async-done(((f32[8,6,256]{2,1,0:T(8,128)}), f32[8,6,256]{2,1,0:T(8,128)S(1)}, u32[]{:S(2)}, u32[]{:S(2)}) %all-to-all-start.2) | async-done | bytes 49184 | tf_op jit(solution)/shard_map/all_to_all | solution.py:51
  63.2 3.5 %all-to-all-start.3 = ((f32[8,6,256]{2,1,0:T(8,128)}), f32[8,6,256]{2,1,0:T(8,128)S(1)}, u32[]{:S(2)}, u32[]{:S(2)}) async-start(f32[8,6,256]{2,1,0:T(8,128)} %all_to_all.57), calls=%async_computation.3 | async-start | bytes 131072 | tf_op jit(solution)/shard_map/all_to_all | solution.py:52
  66.8 1.0 broadcast_multiply_fusion.1
  68.4 5.1 %all-to-all-done.3 = f32[8,6,256]{2,1,0:T(8,128)S(1)} async-done(((f32[8,6,256]{2,1,0:T(8,128)}), f32[8,6,256]{2,1,0:T(8,128)S(1)}, u32[]{:S(2)}, u32[]{:S(2)}) %all-to-all-start.3) | async-done | bytes 49184 | tf_op jit(solution)/shard_map/all_to_all | solution.py:52
  74.1 2.0 %subtract_multiply_fusion = f32[1024,256]{1,0:T(8,128)S(1)} fusion(f32[1024,256]{1,0:T(8,128)S(1)} %fusion.50, f32[1024,256]{1,0:T(8,128)} %fusion.21, f32[1024]{0:T(1024)S(1)} %fusion.84, f32[726,256]{1,0:T(8,128)} %slice_add_fusion.1, f32[42,256]{1,0:T(8,128)S(1)} %fusion.70, f32[256,256]{1,0:T(8,128)S(1)} %broadcast_multiply_fusion.1, ...), kind=kLoop, calls=%fused_computation.57 | loop fusion | flops 2359296 | bytes 5246976 | tf_op jit(solution)/shard_map/mul | solution.py:57
  76.1 0.7 copy-done.1
  76.8 5.9 %fusion.30 = f32[1024,256]{1,0:T(8,128)S(1)} fusion(f32[1,1,1024,1024]{3,2,1,0:T(8,128)S(1)} %copy-done.1, f32[1,1,1024,256]{3,2,1,0:T(8,128)} %param.12, f32[1024,256]{1,0:T(8,128)S(1)} %subtract_multiply_fusion, f32[1024]{0:T(1024)S(1)} %bitcast.152, f32[1024]{0:T(1024)S(1)} %fusion.84, f32[726,256]{1,0:T(8,128)} %slice_add_fusion.1, ...), kind=kOutput, calls=%fused_computation.26 | convolution fusion | flops 3226730496 | bytes 9445376 | tf_op jit(solution)/shard_map/dot_general | solution.py:19
  82.7 0.7 scatter_custom_fusion.5
  83.5 1.3 %scatter_custom_fusion.4 = f32[48,256]{1,0:T(8,128)} fusion(s32[42]{0:T(128)S(1)} %fusion.85, f32[1024,256]{1,0:T(8,128)S(1)} %fusion.30, f32[]{:T(128)} %constant.5.clone.1), kind=kCustom, calls=%fused_computation.76 | custom fusion | bytes 98308 | tf_op jit(solution)/shard_map/scatter | solution.py:49
  84.8 1.0 slice_add_fusion
  85.8 1.4 %all_to_all.60 = f32[8,6,256]{2,1,0:T(8,128)} reshape(f32[48,256]{1,0:T(8,128)} %scatter_custom_fusion.4) | data formatting | bytes 98304 | tf_op jit(solution)/shard_map/all_to_all | solution.py:51
  87.2 4.0 %all-to-all-start.4 = ((f32[8,6,256]{2,1,0:T(8,128)}), f32[8,6,256]{2,1,0:T(8,128)}, u32[]{:S(2)}, u32[]{:S(2)}) async-start(f32[8,6,256]{2,1,0:T(8,128)} %all_to_all.60), calls=%async_computation.4 | async-start | bytes 131072 | tf_op jit(solution)/shard_map/all_to_all | solution.py:51
  91.9 2.3 %all-gather.2 = f32[512,256]{1,0:T(8,128)} all-gather(f32[256,256]{1,0:T(8,128)S(1)} %slice.141), channel_id=4, replica_groups=mesh['grp'=2,'area'=8,'ctg'=2] {'ctg'}, dimensions={0}, use_global_device_ids=true | all-gather | bytes 786432 | tf_op jit(solution)/shard_map/all_gather | solution.py:47
  94.2 1.8 %reduce_sum.42 = f32[256,256]{1,0:T(8,128)} reduce(f32[2,256,256]{2,1,0:T(8,128)} %bitcast.146, f32[]{:T(128)} %constant.5.clone.1), dimensions={0}, to_apply=%region_7.8 | reduce | flops 65536 | bytes 786436 | tf_op jit(solution)/shard_map/reduce_sum | solution.py:47
  96.0 2.2 %all-to-all-done.4 = f32[8,6,256]{2,1,0:T(8,128)} async-done(((f32[8,6,256]{2,1,0:T(8,128)}), f32[8,6,256]{2,1,0:T(8,128)}, u32[]{:S(2)}, u32[]{:S(2)}) %all-to-all-start.4) | async-done | bytes 49184 | tf_op jit(solution)/shard_map/all_to_all | solution.py:51
  98.1 4.0 %all-to-all-start.5 = ((f32[8,6,256]{2,1,0:T(8,128)}), f32[8,6,256]{2,1,0:T(8,128)}, u32[]{:S(2)}, u32[]{:S(2)}) async-start(f32[8,6,256]{2,1,0:T(8,128)} %all_to_all.63), calls=%async_computation.5 | async-start | bytes 131072 | tf_op jit(solution)/shard_map/all_to_all | solution.py:52
  102.1 1.8 %broadcast_multiply_fusion = (f32[256,256]{1,0:T(8,128)}, f32[1,1,256,256]{3,2,1,0:T(8,128)}) fusion(f32[256,256]{1,0:T(8,128)} %reduce_sum.42), kind=kLoop, calls=%fused_computation.71 | loop fusion | flops 65536 | bytes 786432 | tf_op jit(solution)/shard_map/div | solution.py:47
  103.9 0.8 all_to_all.62
  104.7 1.2 %gather_fusion.4 = f32[42,256]{1,0:T(8,128)} fusion(f32[48,256]{1,0:T(8,128)S(1)} %all_to_all.62, s32[1024]{0:T(1024)S(1)} %pad_clamp_fusion), kind=kCustom, calls=%fused_computation.4 | custom fusion | bytes 86184 | tf_op jit(solution)/shard_map/gather | solution.py:53
  106.0 3.1 %all-to-all-done.5 = f32[8,6,256]{2,1,0:T(8,128)} async-done(((f32[8,6,256]{2,1,0:T(8,128)}), f32[8,6,256]{2,1,0:T(8,128)}, u32[]{:S(2)}, u32[]{:S(2)}) %all-to-all-start.5) | async-done | bytes 49184 | tf_op jit(solution)/shard_map/all_to_all | solution.py:52
  109.0 0.8 all_to_all.65
  109.9 1.2 %gather_fusion.5 = f32[42,256]{1,0:T(8,128)} fusion(f32[48,256]{1,0:T(8,128)S(1)} %all_to_all.65, s32[1024]{0:T(1024)S(1)} %pad_clamp_fusion), kind=kCustom, calls=%fused_computation.5 | custom fusion | bytes 86184 | tf_op jit(solution)/shard_map/gather | solution.py:53
  111.1 0.9 fusion.65
  112.0 2.5 %fusion.43 = f32[1,1,1024,256]{3,2,1,0:T(8,128)} fusion(f32[726,256]{1,0:T(8,128)} %slice_add_fusion, f32[42,256]{1,0:T(8,128)S(1)} %fusion.65, f32[256,256]{1,0:T(8,128)} %get-tuple-element.8, f32[1,1024,256]{2,1,0:T(8,128)S(1)} %copy-done.2, f32[1024,256]{1,0:T(8,128)S(1)} %subtract_multiply_fusion, f32[1024,256]{1,0:T(8,128)S(1)} %fusion.30, ...), kind=kLoop, calls=%fused_computation.41 | loop fusion | flops 2359296 | bytes 5246976 | tf_op jit(solution)/shard_map/broadcast_in_dim | solution.py:58
  114.5 1.3 %fusion.38 = f32[1,1,1024,256]{3,2,1,0:T(8,128)} fusion(f32[1,1,726,256]{3,2,1,0:T(8,128)S(1)} %bitcast.145, f32[1,1,42,256]{3,2,1,0:T(8,128)S(1)} %bitcast.149, f32[1,1,256,256]{3,2,1,0:T(8,128)S(1)} %copy-done.8, f32[1,1024,256]{2,1,0:T(8,128)S(1)} %copy-done.2, f32[1024]{0:T(1024)S(1)} %fusion.84), kind=kLoop, calls=%fused_computation.35 | loop fusion | flops 1572864 | bytes 3149824 | tf_op jit(solution)/shard_map/mul | solution.py:56
  (40 shorter events, 5.3 us)
Async XLA Ops:
  3.7 21.8 %all-to-all-start.1 = ((f32[8,6,256]{2,1,0:T(8,128)}), f32[8,6,256]{2,1,0:T(8,128)S(1)}, u32[]{:S(2)}, u32[]{:S(2)}) async-start(f32[8,6,256]{2,1,0:T(8,128)} %all_to_all.51), calls=%async_computation.1 | async-start | bytes 131072 | tf_op jit(solution)/shard_map/all_to_all | solution.py:52
  11.7 7.8 %copy-start.3 = (f32[1,1,1024,256]{3,2,1,0:T(8,128)S(1)}, f32[1,1,1024,256]{3,2,1,0:T(8,128)}, u32[]{:S(2)}) copy-start(f32[1,1,1024,256]{3,2,1,0:T(8,128)} %param.14) | copy-start | bytes 3145732
  19.5 19.6 %copy-start.4 = (f32[1024,256]{1,0:T(8,128)}, f32[1024,256]{1,0:T(8,128)S(1)}, u32[]{:S(2)}) copy-start(f32[1024,256]{1,0:T(8,128)S(1)} %fusion.12) | copy-start | bytes 3145732
  19.5 20.6 %copy-start.2 = (f32[1,1024,256]{2,1,0:T(8,128)S(1)}, f32[1,1024,256]{2,1,0:T(8,128)}, u32[]{:S(2)}) copy-start(f32[1,1024,256]{2,1,0:T(8,128)} %param.15) | copy-start | bytes 3145732
  19.6 0.7 copy-start.7
  22.5 20.0 %copy-start.9 = (f32[1,1,1024]{2,1,0:T(1,128)S(1)}, f32[1,1,1024]{2,1,0:T(1,128)}, u32[]{:S(2)}) copy-start(f32[1,1,1024]{2,1,0:T(1,128)} %param.10) | copy-start | bytes 12292
  25.6 12.9 %all-to-all-start = ((f32[8,6,256]{2,1,0:T(8,128)}), f32[8,6,256]{2,1,0:T(8,128)S(1)}, u32[]{:S(2)}, u32[]{:S(2)}) async-start(f32[8,6,256]{2,1,0:T(8,128)} %all_to_all.48), calls=%async_computation | async-start | bytes 131072 | tf_op jit(solution)/shard_map/all_to_all | solution.py:51
  39.1 3.4 %copy-start = (f32[1,1,1024,1024]{3,2,1,0:T(8,128)S(1)}, f32[1,1,1024,1024]{3,2,1,0:T(8,128)}, u32[]{:S(2)}) copy-start(f32[1,1,1024,1024]{3,2,1,0:T(8,128)} %param.11) | copy-start | bytes 12582916
  39.1 3.4 %copy-start.5 = (f32[1,1,1024,256]{3,2,1,0:T(8,128)S(1)}, f32[1,1,1024,256]{3,2,1,0:T(8,128)}, u32[]{:S(2)}) copy-start(f32[1,1,1024,256]{3,2,1,0:T(8,128)} %param.12) | copy-start | bytes 3145732
  53.0 10.2 %all-to-all-start.2 = ((f32[8,6,256]{2,1,0:T(8,128)}), f32[8,6,256]{2,1,0:T(8,128)S(1)}, u32[]{:S(2)}, u32[]{:S(2)}) async-start(f32[8,6,256]{2,1,0:T(8,128)} %all_to_all.54), calls=%async_computation.2 | async-start | bytes 131072 | tf_op jit(solution)/shard_map/all_to_all | solution.py:51
  63.2 10.2 %all-to-all-start.3 = ((f32[8,6,256]{2,1,0:T(8,128)}), f32[8,6,256]{2,1,0:T(8,128)S(1)}, u32[]{:S(2)}, u32[]{:S(2)}) async-start(f32[8,6,256]{2,1,0:T(8,128)} %all_to_all.57), calls=%async_computation.3 | async-start | bytes 131072 | tf_op jit(solution)/shard_map/all_to_all | solution.py:52
  74.0 2.7 %copy-start.1 = (f32[1,1,1024,1024]{3,2,1,0:T(8,128)S(1)}, f32[1,1,1024,1024]{3,2,1,0:T(8,128)}, u32[]{:S(2)}) copy-start(f32[1,1,1024,1024]{3,2,1,0:T(8,128)} %param.11) | copy-start | bytes 12582916
  87.2 10.9 %all-to-all-start.4 = ((f32[8,6,256]{2,1,0:T(8,128)}), f32[8,6,256]{2,1,0:T(8,128)}, u32[]{:S(2)}, u32[]{:S(2)}) async-start(f32[8,6,256]{2,1,0:T(8,128)} %all_to_all.60), calls=%async_computation.4 | async-start | bytes 131072 | tf_op jit(solution)/shard_map/all_to_all | solution.py:51
  98.1 10.9 %all-to-all-start.5 = ((f32[8,6,256]{2,1,0:T(8,128)}), f32[8,6,256]{2,1,0:T(8,128)}, u32[]{:S(2)}, u32[]{:S(2)}) async-start(f32[8,6,256]{2,1,0:T(8,128)} %all_to_all.63), calls=%async_computation.5 | async-start | bytes 131072 | tf_op jit(solution)/shard_map/all_to_all | solution.py:52
  111.1 3.5 %copy-start.6 = (f32[726,256]{1,0:T(8,128)S(1)}, f32[726,256]{1,0:T(8,128)}, u32[]{:S(2)}) copy-start(f32[726,256]{1,0:T(8,128)} %slice_add_fusion) | copy-start | bytes 2230276
  111.1 3.5 %copy-start.8 = (f32[1,1,256,256]{3,2,1,0:T(8,128)S(1)}, f32[1,1,256,256]{3,2,1,0:T(8,128)}, u32[]{:S(2)}) copy-start(f32[1,1,256,256]{3,2,1,0:T(8,128)} %get-tuple-element.9) | copy-start | bytes 786436
